TPU v7x, 128 devices: a whole 4x4x4 slice. The times are simulated.
128 devices in a mesh: wrap: 16 (over y_hi, x, core), span: 8 (over z, y_lo).
Axes of the slice: x: 4, y: 4 (y_hi: 2, y_lo: 2; y = y_hi * 2 + y_lo), z: 4, core: 2. Of those that a mesh axis runs over, the one named last changes fastest.
Arguments:
- density: float32 [256, 16, 1024], P('wrap', None, 'span'), may hold values from 0.8 to 1.2
- velocity: float32 [3, 256, 16, 1024], P(None, 'wrap', None, 'span'), may hold values from -0.4 to 0.4
- pressure: float32 [256, 16, 1024], P('wrap', None, 'span'), may hold values from 0.7 to 1.4
- metrics: float32 [9, 256, 16, 1024], P(None, 'wrap', None, 'span'), may hold values from -0.3 to 0.3
- volume: float32 [256, 16, 1024], P('wrap', None, 'span'), may hold values from 0.5 to 2
- wake_partner: int32 [256], P('wrap'), may hold values from 0 to 255, as said below
- iblank: int32 [256, 16, 1024], P('wrap', None, 'span'), may hold values 0 or 1
Outputs:
- final_state: float32 [5, 256, 16, 1024], P(None, 'wrap', None, 'span')
Inputs may be any that keep to these rules, and one draw needn't show every extreme that they name: For i in i-slab s (rows s * 16 to (s + 1) * 16 - 1, s from 0), wake_partner[i] is one of the rows (n - 1 - s) * 16 to (n - s) * 16 - 1 with n = 16; each of those rows is named once.
All inputs are finite; a program needn't handle non-finite values. No bound on the sum of `iblank` on one device may be relied on, other than what follows from the above.
Results may differ from a plain program's by a relative error of at most 0.0003.
Values sent between devices are 32-bit elements; how exact they have to be, the bound alone decides.
A program may use at most 64 MiB of HBM per device.

v0:
```python
import jax
import jax.numpy as jnp
from jax import lax
from jax.experimental import pallas as pl
from jax.experimental.pallas import tpu as pltpu
from jax.sharding import PartitionSpec as P

MESH = pl.DeviceIdType.MESH
F32 = jnp.float32
CELLS = 16
POINTS = CELLS + 6
ROWS = 256
LANES = 128
PLANE = 16
HALO = 3 * PLANE
PADDED = ROWS + 2 * HALO
KROWS = LANES + 16
TIME_STEP = 0.05


def point_terms(prims, metric, direction):
    rho, u, v, w, pressure = prims
    x = list(metric)
    x[direction] = x[direction] + 1.0
    temperature = pressure / rho
    half_sq = 0.5 * (u * u + v * v + w * w)
    contra = x[0] * u + x[1] * v + x[2] * w
    metric_sq = x[0] * x[0] + x[1] * x[1] + x[2] * x[2]
    wave = jnp.abs(contra) + jnp.sqrt(1.4 * temperature * metric_sq)
    energy = 2.5 * pressure + rho * half_sq
    mass_flux = rho * contra
    mass_wave = rho * wave
    plus, minus = [], []
    fluxes = [mass_flux] + [mass_flux * vel + x[m] * pressure for m, vel in enumerate((u, v, w))]
    fluxes.append((energy + pressure) * contra)
    spread = [mass_wave, mass_wave * u, mass_wave * v, mass_wave * w, wave * energy]
    plus = [f + s for f, s in zip(fluxes, spread)]
    minus = [f - s for f, s in zip(fluxes, spread)]
    return plus + minus + [u, v, w, half_sq + temperature, 1.6 * metric_sq]


def smoothness(before, after):
    curve = after - before
    slope = after + before
    curve4 = 4.0 * curve
    square = curve4 * curve
    middle = square * (13.0 / 12.0) + (slope * slope + 16e-6)
    sides = middle + square
    cross = curve4 * slope
    left = sides + cross
    right = sides - cross
    return curve * (1.0 / 3.0), slope, left * left, middle * middle, right * right


def blend(first, second, third, far, near):
    near_sum = third + second
    total = second * third + first * near_sum
    return second * (third * far + first * near) / total


def line_sweep(load, viscous, store):
    state = []
    for sign in range(2):
        state.append({"v": load(sign, 1), "d": None})
        state[sign]["d"] = state[sign]["v"] - load(sign, 0)
    history = [[], []]
    slopes = {}
    plus_face = {}
    face_before = None
    for p in range(1, POINTS - 1):
        for sign in range(2):
            now = state[sign]
            ahead = load(sign, p + 1)
            after = ahead - now["v"]
            curve, slope, left, middle, right = smoothness(now["d"], after)
            now["v"], now["d"] = ahead, after
            history[sign].append((curve, left, middle, right))
            if len(history[sign]) > 4:
                history[sign].pop(0)
            slopes[p] = slope if sign == 0 else slopes[p] + slope
        if p >= 3:
            face = p - 3
            if face <= CELLS:
                (c0, l0, _, _), (c1, _, m1, _), (c2, _, _, r2) = history[0][-3:]
                plus_face[face] = c1 + blend(6.0 * l0, m1, 2.0 * r2, 2.0 * (c1 - c0), c2 - c1)
        if p >= 4:
            face = p - 4
            (c2, l2, _, _), (c1, _, m1, _), (c0, _, _, r0) = history[1][-3:]
            value = plus_face.pop(face) + (
                c1 - blend(6.0 * r0, m1, 2.0 * l2, 2.0 * (c0 - c1), c1 - c2)
            )
            if viscous is not None:
                value = value + viscous(face)
            if face >= 1:
                store(face - 1, value - face_before - slopes.pop(face + 2))
            face_before = value


def kernel(
    rho_hbm, vel_hbm, prs_hbm, met_hbm, vol_hbm, blank_hbm, partner_ref, out_ref,
    prims_a, prims_b, chord, normal, span_rows, volume, blank, coef,
    wake_send_a, wake_send_b, wake_recv_a, wake_recv_b, wake_rows,
    spans_a, spans_b, span_metric, terms, net_i, net_j, net_k, half, result,
    local_sem, send_sem, recv_sem, out_sem,
):
    wrap, wraps = lax.axis_index("wrap"), lax.axis_size("wrap")
    span, spans = lax.axis_index("span"), lax.axis_size("span")
    up, down = lax.rem(span + 1, spans), lax.rem(span + spans - 1, spans)
    mirror = wraps - 1 - wrap
    has_left, has_right = wrap > 0, wrap < wraps - 1
    left = {"wrap": jnp.maximum(wrap - 1, 0)}
    right = {"wrap": jnp.minimum(wrap + 1, wraps - 1)}
    own = pl.ds(HALO, ROWS)

    loads = [
        pltpu.make_async_copy(src, dst, local_sem.at[n])
        for n, (src, dst) in enumerate(
            [
                (rho_hbm, prims_a.at[0, own]),
                (vel_hbm, prims_a.at[pl.ds(1, 3), own]),
                (prs_hbm, prims_a.at[4, own]),
                (met_hbm.at[pl.ds(6, 3)], span_rows),
                (met_hbm.at[pl.ds(0, 3)], chord.at[:, own]),
                (met_hbm.at[pl.ds(3, 3)], normal),
                (vol_hbm, volume),
                (blank_hbm, blank),
            ]
        )
    ]
    for load in loads:
        load.start()

    barrier = pltpu.get_barrier_semaphore()
    for target in ({"span": up}, {"span": down}, {"wrap": mirror}):
        pl.semaphore_signal(barrier, inc=1, device_id=target, device_id_type=MESH)

    @pl.when(has_left)
    def _():
        pl.semaphore_signal(barrier, inc=1, device_id=left, device_id_type=MESH)

    @pl.when(has_right)
    def _():
        pl.semaphore_signal(barrier, inc=1, device_id=right, device_id_type=MESH)

    pl.semaphore_wait(barrier, 3 + has_left.astype(jnp.int32) + has_right.astype(jnp.int32))

    def remote(src, dst, n, target):
        return pltpu.make_async_remote_copy(
            src_ref=src, dst_ref=dst, send_sem=send_sem.at[n], recv_sem=recv_sem.at[n],
            device_id=target, device_id_type=MESH,
        )

    first, last = pl.ds(0, HALO), pl.ds(ROWS - HALO, HALO)
    low, high = pl.ds(0, HALO), pl.ds(HALO + ROWS, HALO)
    three = pl.ds(1, 3)
    to_right_a = [
        remote(rho_hbm.at[last], prims_a.at[0, low], 0, right),
        remote(vel_hbm.at[:, last], prims_a.at[three, low], 1, right),
        remote(prs_hbm.at[last], prims_a.at[4, low], 2, right),
        remote(met_hbm.at[pl.ds(0, 3), last], chord.at[:, low], 3, right),
    ]
    to_left_a = [
        remote(rho_hbm.at[first], prims_a.at[0, high], 4, left),
        remote(vel_hbm.at[:, first], prims_a.at[three, high], 5, left),
        remote(prs_hbm.at[first], prims_a.at[4, high], 6, left),
        remote(met_hbm.at[pl.ds(0, 3), first], chord.at[:, high], 7, left),
    ]
    wake_a = remote(wake_send_a, wake_recv_a, 8, {"wrap": mirror})
    bottom, top = pl.ds(8, 8), pl.ds(LANES, 8)
    below, above = pl.ds(0, 8), pl.ds(8 + LANES, 8)
    spans_1 = [
        remote(spans_a.at[:, :, top], spans_a.at[:, :, below], 9, {"span": up}),
        remote(span_metric.at[:, :, top], span_metric.at[:, :, below], 10, {"span": up}),
        remote(spans_a.at[:, :, bottom], spans_a.at[:, :, above], 11, {"span": down}),
        remote(span_metric.at[:, :, bottom], span_metric.at[:, :, above], 12, {"span": down}),
    ]
    to_right_b = [remote(prims_b.at[:, pl.ds(ROWS, HALO)], prims_b.at[:, low], 13, right)]
    to_left_b = [remote(prims_b.at[:, pl.ds(HALO, HALO)], prims_b.at[:, high], 14, left)]
    wake_b = remote(wake_send_b, wake_recv_b, 15, {"wrap": mirror})
    spans_2 = [
        remote(spans_b.at[:, :, top], spans_b.at[:, :, below], 16, {"span": up}),
        remote(spans_b.at[:, :, bottom], spans_b.at[:, :, above], 17, {"span": down}),
    ]

    def start_sides(to_left, to_right):
        @pl.when(has_right)
        def _():
            for copy in to_right:
                copy.start()

        @pl.when(has_left)
        def _():
            for copy in to_left:
                copy.start()

    def finish_sides(to_left, to_right, arrays):
        @pl.when(has_left)
        def _():
            for copy in to_right:
                copy.wait_recv()

        @pl.when(has_right)
        def _():
            for copy in to_left:
                copy.wait_recv()

        @pl.when(jnp.logical_not(has_left))
        def _():
            for array, count in arrays:
                for m in range(count):
                    edge = array[m, HALO : HALO + PLANE, :]
                    for n in range(3):
                        array[m, n * PLANE : (n + 1) * PLANE, :] = edge

        @pl.when(jnp.logical_not(has_right))
        def _():
            for array, count in arrays:
                for m in range(count):
                    edge = array[m, HALO + ROWS - PLANE : HALO + ROWS, :]
                    for n in range(3):
                        start = HALO + ROWS + n * PLANE
                        array[m, start : start + PLANE, :] = edge

    def drain_sides(to_left, to_right):
        @pl.when(has_right)
        def _():
            for copy in to_right:
                copy.wait_send()

        @pl.when(has_left)
        def _():
            for copy in to_left:
                copy.wait_send()

    def pack_wake(prims, send):
        flat_send = send.reshape(ROWS, LANES)
        for m in range(5):
            for r in range(3):
                for h in range(2):
                    rows = prims[m, pl.ds(HALO + 128 * h + 1 + r, 8, stride=16), :]
                    flat_send[pl.ds(128 * h + 3 * m + r, 8, stride=16), :] = rows

    def unpack_wake(recv):
        slab = mirror * CELLS
        for i in range(CELLS):
            wake_rows[i * 16 : (i + 1) * 16, :] = recv[jnp.clip(partner_ref[i] - slab, 0, CELLS - 1)]

    def turn(src, dst, count, base):
        def body(n, carry):
            m, t = n // 2, lax.rem(n, 2)
            start = pl.multiple_of(base + 128 * t, 16)
            dst[m, t, 8 : 8 + LANES, :] = src[m, pl.ds(start, LANES), :].T
            return carry

        lax.fori_loop(0, 2 * count, body, 0)

    def put_terms(direction, p, h, values):
        for f, value in enumerate(values):
            terms[direction, f, 2 * p + h] = value

    def points_i(prims, begin, end):
        def body(p, carry):
            for h in range(2):
                rows = pl.ds(pl.multiple_of(p * PLANE + 8 * h, 8), 8)
                values = point_terms(
                    [prims[m, rows, :] for m in range(5)], [chord[m, rows, :] for m in range(3)], 0
                )
                put_terms(0, p, h, values)
            return carry

        lax.fori_loop(begin, end, body, 0)

    def points_j(prims, begin, end):
        def body(p, carry):
            for h in range(2):
                j = jnp.clip(p - 3, 0, CELLS - 1)
                rows = pl.ds(HALO + 128 * h + j, 8, stride=16)
                metric_rows = pl.ds(128 * h + j, 8, stride=16)
                values = point_terms(
                    [prims[m, rows, :] for m in range(5)],
                    [normal[m, metric_rows, :] for m in range(3)],
                    1,
                )
                put_terms(1, p, h, values)
            return carry

        lax.fori_loop(begin, end, body, 0)

    def points_wake():
        for p in range(3):
            for h in range(2):
                values = point_terms(
                    [wake_rows[pl.ds(128 * h + 3 * m + 2 - p, 8, stride=16), :] for m in range(5)],
                    [normal[m, pl.ds(128 * h, 8, stride=16), :] for m in range(3)],
                    1,
                )
                put_terms(1, p, h, values)

    def points_k(array):
        def body(p, carry):
            for h in range(2):
                rows = pl.ds(5 + p, 8, stride=16)
                values = point_terms(
                    [array[m, h, rows, :] for m in range(5)],
                    [span_metric[m, h, rows, :] for m in range(3)],
                    2,
                )
                put_terms(2, p, h, values)
            return carry

        lax.fori_loop(0, POINTS, body, 0)

    def sweep(direction, put):
        def one(m, h, with_viscous):
            def load(sign, p):
                return terms[direction, 5 * sign + m, 2 * p + h]

            def viscous(face):
                a, b = 2 * (face + 2) + h, 2 * (face + 3) + h
                scale = terms[direction, 14, a] + terms[direction, 14, b]
                return scale * (terms[direction, 9 + m, b] - terms[direction, 9 + m, a])

            line_sweep(load, viscous if with_viscous else None, lambda n, v: put(m, h, n, v))

        def mass(h, carry):
            one(0, h, False)
            return carry

        def others(n, carry):
            one(1 + n // 2, lax.rem(n, 2), True)
            return carry

        lax.fori_loop(0, 2, mass, 0)
        lax.fori_loop(0, 8, others, 0)

    def put_i(m, h, n, value):
        net_i[m, pl.ds(pl.multiple_of(n * PLANE + 8 * h, 8), 8), :] = value

    def put_j(m, h, n, value):
        net_j[m, pl.ds(128 * h + n, 8, stride=16), :] = value

    def put_k(m, h, n, value):
        net_k[m, h, pl.ds(n, 8, stride=16), :] = value

    def turn_back():
        def body(n, carry):
            m, t = n // 2, lax.rem(n, 2)
            rows = pl.ds(pl.multiple_of(128 * t, 128), LANES)
            net_i[m, rows, :] = net_i[m, rows, :] + net_j[m, rows, :] + net_k[m, t].T
            return carry

        lax.fori_loop(0, 10, body, 0)

    def update_first(n, carry):
        rows = pl.ds(pl.multiple_of(8 * n, 8), 8)
        at = pl.ds(pl.multiple_of(HALO + 8 * n, 8), 8)
        rho, u, v, w, pressure = [prims_a[m, at, :] for m in range(5)]
        scale = coef[rows, :]
        energy = 2.5 * pressure + 0.5 * rho * (u * u + v * v + w * w)
        before = [rho, rho * u, rho * v, rho * w, energy]
        after = [b + scale * net_i[m, rows, :] for m, b in enumerate(before)]
        for m in range(5):
            half[m, rows, :] = 0.5 * (before[m] + after[m])
        vel = [after[m] / after[0] for m in (1, 2, 3)]
        speed_sq = vel[0] * vel[0] + vel[1] * vel[1] + vel[2] * vel[2]
        prims_b[0, at, :] = after[0]
        for m in range(3):
            prims_b[1 + m, at, :] = vel[m]
        prims_b[4, at, :] = 0.4 * (after[4] - 0.5 * after[0] * speed_sq)
        return carry

    def update_second(n, carry):
        rows = pl.ds(pl.multiple_of(8 * n, 8), 8)
        scale = 0.5 * coef[rows, :]
        for m in range(5):
            result[m, rows, :] = half[m, rows, :] + scale * net_i[m, rows, :]
        return carry

    start_sides(to_left_a, to_right_a)
    for load in loads[:4]:
        load.wait()
    pack_wake(prims_a, wake_send_a)
    wake_a.start()
    turn(prims_a, spans_a, 5, HALO)
    turn(span_rows, span_metric, 3, 0)
    for copy in spans_1:
        copy.start()
    for load in loads[4:]:
        load.wait()

    def scale_rows(n, carry):
        rows = pl.ds(pl.multiple_of(8 * n, 8), 8)
        coef[rows, :] = (0.25 * TIME_STEP) * blank[rows, :].astype(F32) / volume[rows, :]
        return carry

    lax.fori_loop(0, ROWS // 8, scale_rows, 0)

    def stage(prims, array, span_copies, to_left, to_right, edges, wake, recv):
        points_i(prims, 3, 3 + CELLS)
        points_j(prims, 3, POINTS)
        for copy in span_copies:
            copy.wait_recv()
        points_k(array)
        sweep(2, put_k)
        finish_sides(to_left, to_right, edges)
        points_i(prims, 0, 3)
        points_i(prims, 3 + CELLS, POINTS)
        sweep(0, put_i)
        wake.wait_recv()
        unpack_wake(recv)
        points_wake()
        sweep(1, put_j)
        turn_back()
        drain_sides(to_left, to_right)
        for copy in span_copies:
            copy.wait_send()
        wake.wait_send()

    stage(
        prims_a, spans_a, spans_1, to_left_a, to_right_a,
        [(prims_a, 5), (chord, 3)], wake_a, wake_recv_a,
    )
    lax.fori_loop(0, ROWS // 8, update_first, 0)
    start_sides(to_left_b, to_right_b)
    pack_wake(prims_b, wake_send_b)
    wake_b.start()
    turn(prims_b, spans_b, 5, HALO)
    for copy in spans_2:
        copy.start()
    stage(
        prims_b, spans_b, spans_2, to_left_b, to_right_b,
        [(prims_b, 5)], wake_b, wake_recv_b,
    )
    lax.fori_loop(0, ROWS // 8, update_second, 0)
    done = pltpu.make_async_copy(result, out_ref, out_sem)
    done.start()
    done.wait()


def body(density, velocity, pressure, metrics, volume, wake_partner, iblank):
    flat = lambda array: array.reshape(array.shape[:-3] + (ROWS, LANES))
    anywhere = pl.BlockSpec(memory_space=pl.ANY)
    out = pl.pallas_call(
        kernel,
        out_shape=jax.ShapeDtypeStruct((5, ROWS, LANES), F32),
        in_specs=[anywhere] * 6 + [pl.BlockSpec(memory_space=pltpu.SMEM)],
        out_specs=anywhere,
        scratch_shapes=[
            pltpu.VMEM((5, PADDED, LANES), F32),
            pltpu.VMEM((5, PADDED, LANES), F32),
            pltpu.VMEM((3, PADDED, LANES), F32),
            pltpu.VMEM((3, ROWS, LANES), F32),
            pltpu.VMEM((3, ROWS, LANES), F32),
            pltpu.VMEM((ROWS, LANES), F32),
            pltpu.VMEM((ROWS, LANES), jnp.int32),
            pltpu.VMEM((ROWS, LANES), F32),
            pltpu.VMEM((CELLS, 16, LANES), F32),
            pltpu.VMEM((CELLS, 16, LANES), F32),
            pltpu.VMEM((CELLS, 16, LANES), F32),
            pltpu.VMEM((CELLS, 16, LANES), F32),
            pltpu.VMEM((ROWS, LANES), F32),
            pltpu.VMEM((5, 2, KROWS, LANES), F32),
            pltpu.VMEM((5, 2, KROWS, LANES), F32),
            pltpu.VMEM((3, 2, KROWS, LANES), F32),
            pltpu.VMEM((3, 15, 2 * POINTS, 8, LANES), F32),
            pltpu.VMEM((5, ROWS, LANES), F32),
            pltpu.VMEM((5, ROWS, LANES), F32),
            pltpu.VMEM((5, 2, LANES, LANES), F32),
            pltpu.VMEM((5, ROWS, LANES), F32),
            pltpu.VMEM((5, ROWS, LANES), F32),
            pltpu.SemaphoreType.DMA((8,)),
            pltpu.SemaphoreType.DMA((18,)),
            pltpu.SemaphoreType.DMA((18,)),
            pltpu.SemaphoreType.DMA,
        ],
        compiler_params=pltpu.CompilerParams(
            collective_id=0, has_side_effects=True, vmem_limit_bytes=63 * 1024 * 1024
        ),
        name="weno_sections",
    )(
        flat(density), flat(velocity), flat(pressure), flat(metrics), flat(volume),
        flat(iblank), wake_partner,
    )
    return out.reshape(5, CELLS, PLANE, LANES)


def solution(mesh):
    placed = (
        P("wrap", None, "span"),
        P(None, "wrap", None, "span"),
        P("wrap", None, "span"),
        P(None, "wrap", None, "span"),
        P("wrap", None, "span"),
        P("wrap"),
        P("wrap", None, "span"),
    )
    return jax.shard_map(
        body, mesh=mesh, in_specs=placed, out_specs=P(None, "wrap", None, "span"), check_vma=False
    )
```

profile of v0, /device:TPU:1, one launch (start us, length us, event | category | flops | bytes accessed | tf_op | source)
XLA Modules:
  0.0 46.5 jit_solution(3994917130218733787)
XLA Ops:
  0.0 44.5 %weno_sections.1 = f32[5,256,128]{2,1,0:T(8,128)} custom-call(f32[256,128]{1,0:T(8,128)} %bitcast.10, f32[3,256,128]{2,1,0:T(8,128)} %bitcast.9, f32[256,128]{1,0:T(8,128)} %bitcast.11, f32[9,256,128]{2,1,0:T(8,128)} %bitcast.8, f32[256,128]{1,0:T(8,128)} %bitcast.12, s32[256,128]{1,0:T(8,128)} %bitcast.13, s32[16]{0:T(128)} %partner_ref.1), custom_call_target="tpu_custom_call" | custom-call | tf_op jit(solution)/shard_map/weno_sections/pallas_call | solution.py:443
  44.6 2.0 %copy.9 = f32[5,16,16,128]{3,2,1,0:T(8,128)} copy(f32[5,16,16,128]{3,2,1,0:T(8,128)} %bitcast.7) | data formatting | bytes 1310720
where the time goes:
time: 46.7 us; the launch traced here: 46.5 us
  Pallas kernels  44.5 us (95%)
  local copies, waits for them, and re-layouts  1.99 us (4%)
    pallas_call x1, Pallas kernels, body(): pl.pallas_call(kernel, out_shape=jax.ShapeDtypeStruct((5, ROWS, LANES), F...  44.5 us
    unnamed x1, local copies, waits for them, and re-layouts  1.99 us

commit v1 on v0

v1 whole, which is shorter than its diff:
```python
import jax
import jax.numpy as jnp
from jax import lax
from jax.experimental import pallas as pl
from jax.experimental.pallas import tpu as pltpu
from jax.sharding import PartitionSpec as P

MESH = pl.DeviceIdType.MESH
F32 = jnp.float32
CELLS = 16
POINTS = CELLS + 6
ROWS = 256
LANES = 128
PLANE = 16
HALO = 3 * PLANE
PADDED = ROWS + 2 * HALO
ODD = PLANE + 1
SPAN_ROWS = 176
TIME_STEP = 0.05


def point_terms(prims, metric, direction):
    rho, u, v, w, pressure = prims
    x = list(metric)
    x[direction] = x[direction] + 1.0
    temperature = pressure / rho
    half_sq = 0.5 * (u * u + v * v + w * w)
    contra = x[0] * u + x[1] * v + x[2] * w
    metric_sq = x[0] * x[0] + x[1] * x[1] + x[2] * x[2]
    wave = jnp.abs(contra) + jnp.sqrt(1.4 * temperature * metric_sq)
    energy = 2.5 * pressure + rho * half_sq
    mass_flux = rho * contra
    mass_wave = rho * wave
    fluxes = [mass_flux] + [mass_flux * vel + x[m] * pressure for m, vel in enumerate((u, v, w))]
    fluxes.append((energy + pressure) * contra)
    spread = [mass_wave, mass_wave * u, mass_wave * v, mass_wave * w, wave * energy]
    plus = [f + s for f, s in zip(fluxes, spread)]
    minus = [f - s for f, s in zip(fluxes, spread)]
    whole = [6.0 * f for f in fluxes]
    return plus + minus + whole + [u, v, w, half_sq + temperature, 4.8 * metric_sq]


def smoothness(before, after):
    curve = after - before
    base = curve * curve * (4.0 / 3.0) + 4e-6
    left = base + after * (after + curve)
    middle = base + after * before
    right = base + before * (before - curve)
    return curve, left * left, middle * middle, right * right


def blend(first, second, third, far, near):
    near_sum = third + second
    total = second * third + first * near_sum
    return second * (third * far + first * near) / total


def line_sweep(load, whole, viscous, store, begin, end):
    state = []
    for sign in range(2):
        value = load(sign, begin + 1)
        state.append([value, value - load(sign, begin)])
    history = [[], []]
    plus_face = {}
    face_before = None
    for p in range(begin + 1, end + 5):
        for sign in range(2):
            value, before = state[sign]
            ahead = load(sign, p + 1)
            after = ahead - value
            history[sign].append(smoothness(before, after))
            state[sign] = [ahead, after]
            if len(history[sign]) > 3:
                history[sign].pop(0)
        face = p - 3
        if begin <= face <= end:
            (c0, l0, _, _), (c1, _, m1, _), (c2, _, _, r2) = history[0]
            plus_face[face] = c1 + blend(6.0 * l0, m1, 2.0 * r2, 2.0 * (c1 - c0), c2 - c1)
        face = p - 4
        if face >= begin:
            (c2, l2, _, _), (c1, _, m1, _), (c0, _, _, r0) = history[1]
            value = plus_face.pop(face) + (
                c1 - blend(6.0 * r0, m1, 2.0 * l2, 2.0 * (c0 - c1), c1 - c2)
            )
            if viscous is not None:
                value = value + viscous(face)
            if face > begin:
                n = face - 1
                store(n, value - face_before - (whole(n + 4) - whole(n + 2)))
            face_before = value


def kernel(
    rho_hbm, vel_hbm, prs_hbm, met_hbm, vol_hbm, blank_hbm, partner_ref, result,
    prims_a, prims_b, prims_j, chord, normal, normal_j, span_rows, volume, blank, coef,
    wake_send_a, wake_send_b, wake_recv_a, wake_recv_b, wake_rows,
    spans, span_metric, pack_up_a, pack_down_a, pack_up_b, pack_down_b,
    below_a, above_a, below_b, above_b,
    terms, net_i, net_j, net_k, turned, half,
    local_sem, send_sem, recv_sem,
):
    wrap, wraps = lax.axis_index("wrap"), lax.axis_size("wrap")
    span, span_count = lax.axis_index("span"), lax.axis_size("span")
    up, down = lax.rem(span + 1, span_count), lax.rem(span + span_count - 1, span_count)
    mirror = wraps - 1 - wrap
    has_left, has_right = wrap > 0, wrap < wraps - 1
    left = {"wrap": jnp.maximum(wrap - 1, 0)}
    right = {"wrap": jnp.minimum(wrap + 1, wraps - 1)}
    own = pl.ds(HALO, ROWS)

    loads = [
        pltpu.make_async_copy(src, dst, local_sem.at[n])
        for n, (src, dst) in enumerate(
            [
                (rho_hbm, prims_a.at[0, own]),
                (vel_hbm, prims_a.at[pl.ds(1, 3), own]),
                (prs_hbm, prims_a.at[4, own]),
                (met_hbm.at[pl.ds(6, 3)], span_rows),
                (met_hbm.at[pl.ds(3, 3)], normal),
                (met_hbm.at[pl.ds(0, 3)], chord.at[:, own]),
                (vol_hbm, volume),
                (blank_hbm, blank),
            ]
        )
    ]
    for load in loads:
        load.start()

    barrier = pltpu.get_barrier_semaphore()
    for target in ({"span": up}, {"span": down}, {"wrap": mirror}):
        pl.semaphore_signal(barrier, inc=1, device_id=target, device_id_type=MESH)

    @pl.when(has_left)
    def _():
        pl.semaphore_signal(barrier, inc=1, device_id=left, device_id_type=MESH)

    @pl.when(has_right)
    def _():
        pl.semaphore_signal(barrier, inc=1, device_id=right, device_id_type=MESH)

    def remote(src, dst, n, target):
        return pltpu.make_async_remote_copy(
            src_ref=src, dst_ref=dst, send_sem=send_sem.at[n], recv_sem=recv_sem.at[n],
            device_id=target, device_id_type=MESH,
        )

    first, last = pl.ds(0, HALO), pl.ds(ROWS - HALO, HALO)
    low, high = pl.ds(0, HALO), pl.ds(HALO + ROWS, HALO)
    three = pl.ds(1, 3)
    to_right_a = [
        remote(rho_hbm.at[last], prims_a.at[0, low], 0, right),
        remote(vel_hbm.at[:, last], prims_a.at[three, low], 1, right),
        remote(prs_hbm.at[last], prims_a.at[4, low], 2, right),
        remote(met_hbm.at[pl.ds(0, 3), last], chord.at[:, low], 3, right),
    ]
    to_left_a = [
        remote(rho_hbm.at[first], prims_a.at[0, high], 4, left),
        remote(vel_hbm.at[:, first], prims_a.at[three, high], 5, left),
        remote(prs_hbm.at[first], prims_a.at[4, high], 6, left),
        remote(met_hbm.at[pl.ds(0, 3), first], chord.at[:, high], 7, left),
    ]
    wake_a = remote(wake_send_a, wake_recv_a, 8, {"wrap": mirror})
    spans_1 = [
        remote(pack_up_a, below_a, 9, {"span": up}),
        remote(pack_down_a, above_a, 10, {"span": down}),
    ]
    to_right_b = [remote(prims_b.at[:, pl.ds(ROWS, HALO)], prims_b.at[:, low], 11, right)]
    to_left_b = [remote(prims_b.at[:, pl.ds(HALO, HALO)], prims_b.at[:, high], 12, left)]
    wake_b = remote(wake_send_b, wake_recv_b, 13, {"wrap": mirror})
    spans_2 = [
        remote(pack_up_b, below_b, 14, {"span": up}),
        remote(pack_down_b, above_b, 15, {"span": down}),
    ]

    def start_sides(to_left, to_right):
        @pl.when(has_right)
        def _():
            for copy in to_right:
                copy.start()

        @pl.when(has_left)
        def _():
            for copy in to_left:
                copy.start()

    def finish_sides(to_left, to_right, arrays):
        @pl.when(has_left)
        def _():
            for copy in to_right:
                copy.wait_recv()

        @pl.when(has_right)
        def _():
            for copy in to_left:
                copy.wait_recv()

        @pl.when(jnp.logical_not(has_left))
        def _():
            for array, count in arrays:
                for m in range(count):
                    edge = array[m, HALO : HALO + PLANE, :]
                    for n in range(3):
                        array[m, n * PLANE : (n + 1) * PLANE, :] = edge

        @pl.when(jnp.logical_not(has_right))
        def _():
            for array, count in arrays:
                for m in range(count):
                    edge = array[m, HALO + ROWS - PLANE : HALO + ROWS, :]
                    for n in range(3):
                        start = HALO + ROWS + n * PLANE
                        array[m, start : start + PLANE, :] = edge

    def drain_sides(to_left, to_right):
        @pl.when(has_right)
        def _():
            for copy in to_right:
                copy.wait_send()

        @pl.when(has_left)
        def _():
            for copy in to_left:
                copy.wait_send()

    def spread_rows(src, base, dst, count):
        for m in range(count):
            for i in range(CELLS):
                rows = src[m, base + PLANE * i : base + PLANE * (i + 1), :]
                dst[m, ODD * i : ODD * i + PLANE, :] = rows

    def pack_wake(prims, send):
        for i in range(CELLS):
            for m in range(5):
                start = HALO + PLANE * i + 1
                send[i, 3 * m : 3 * m + 3, :] = prims[m, start : start + 3, :]

    def unpack_wake(recv):
        slab = mirror * CELLS
        for i in range(CELLS):
            rows = recv[jnp.clip(partner_ref[i] - slab, 0, CELLS - 1)]
            wake_rows[ODD * i : ODD * i + PLANE, :] = rows

    def turn(src, dst, count, base):
        for m in range(count):
            for t in range(2):
                block = src[m, base + LANES * t : base + LANES * (t + 1), :].T
                for q in range(8):
                    start = ODD * (q + 1)
                    dst[m, t, start : start + CELLS, :] = block[CELLS * q : CELLS * (q + 1), :]

    def pack_spans(arrays, pack_up, pack_down):
        n = 0
        for array, count in arrays:
            for m in range(count):
                for t in range(2):
                    pack_up[n : n + 3, :] = array[m, t, 8 * ODD + 13 : 8 * ODD + 16, :]
                    pack_down[n : n + 3, :] = array[m, t, ODD : ODD + 3, :]
                    n += 3

    def unpack_spans(arrays, below, above):
        n = 0
        for array, count in arrays:
            for m in range(count):
                for t in range(2):
                    array[m, t, 13:16, :] = below[n : n + 3, :]
                    array[m, t, 9 * ODD : 9 * ODD + 3, :] = above[n : n + 3, :]
                    n += 3

    def put_terms(direction, p, h, values):
        for f, value in enumerate(values):
            terms[direction, f, 2 * p + h] = value

    def points_i(prims, begin, end, unroll):
        def body(p, carry):
            for h in range(2):
                rows = pl.ds(pl.multiple_of(p * PLANE + 8 * h, 8), 8)
                values = point_terms(
                    [prims[m, rows, :] for m in range(5)], [chord[m, rows, :] for m in range(3)], 0
                )
                put_terms(0, p, h, values)
            return carry

        lax.fori_loop(begin, end, body, 0, unroll=unroll)

    def points_j():
        def at(j, h):
            rows = pl.ds(ODD * 8 * h + j, 8, stride=ODD)
            return point_terms(
                [prims_j[m, rows, :] for m in range(5)], [normal_j[m, rows, :] for m in range(3)], 1
            )

        def body(j, carry):
            for h in range(2):
                put_terms(1, j + 3, h, at(j, h))
            return carry

        lax.fori_loop(0, CELLS - 2, body, 0, unroll=2)
        for h in range(2):
            put_terms(1, CELLS + 1, h, at(CELLS - 2, h))
            values = at(CELLS - 1, h)
            for p in range(CELLS + 2, POINTS):
                put_terms(1, p, h, values)

    def points_wake():
        for p in range(3):
            for h in range(2):
                values = point_terms(
                    [
                        wake_rows[pl.ds(ODD * 8 * h + 3 * m + 2 - p, 8, stride=ODD), :]
                        for m in range(5)
                    ],
                    [normal_j[m, pl.ds(ODD * 8 * h, 8, stride=ODD), :] for m in range(3)],
                    1,
                )
                put_terms(1, p, h, values)

    def points_k(begin, end, shift, unroll):
        def body(p, carry):
            for h in range(2):
                rows = pl.ds(p + shift, 8, stride=ODD)
                values = point_terms(
                    [spans[m, h, rows, :] for m in range(5)],
                    [span_metric[m, h, rows, :] for m in range(3)],
                    2,
                )
                put_terms(2, p, h, values)
            return carry

        lax.fori_loop(begin, end, body, 0, unroll=unroll)

    def sweep(direction, put, begin=0, end=CELLS):
        def one(m, h, with_viscous):
            def load(sign, p):
                return terms[direction, 5 * sign + m, 2 * p + h]

            def whole(p):
                return terms[direction, 10 + m, 2 * p + h]

            def viscous(face):
                a, b = 2 * (face + 2) + h, 2 * (face + 3) + h
                scale = terms[direction, 19, a] + terms[direction, 19, b]
                return scale * (terms[direction, 14 + m, b] - terms[direction, 14 + m, a])

            line_sweep(
                load, whole, viscous if with_viscous else None,
                lambda n, v: put(m, h, n, v), begin, end,
            )

        def mass(h, carry):
            one(0, h, False)
            return carry

        def others(n, carry):
            one(1 + n // 2, lax.rem(n, 2), True)
            return carry

        lax.fori_loop(0, 2, mass, 0)
        lax.fori_loop(0, 8, others, 0)

    def put_i(m, h, n, value):
        net_i[m, pl.ds(pl.multiple_of(n * PLANE + 8 * h, 8), 8), :] = value

    def put_j(m, h, n, value):
        net_j[m, pl.ds(ODD * 8 * h + n, 8, stride=ODD), :] = value

    def put_k(m, h, n, value):
        net_k[m, h, pl.ds(n, 8, stride=ODD), :] = value

    def turn_back():
        for m in range(5):
            for t in range(2):
                parts = [net_k[m, t, ODD * q : ODD * q + CELLS, :] for q in range(8)]
                turned[m, LANES * t : LANES * (t + 1), :] = jnp.concatenate(parts, axis=0).T

    def whole_net(m, i, h, rows):
        return net_i[m, rows, :] + net_j[m, pl.ds(ODD * i + 8 * h, 8), :] + turned[m, rows, :]

    def update_first(i, carry):
        for h in range(2):
            rows = pl.ds(pl.multiple_of(PLANE * i + 8 * h, 8), 8)
            at = pl.ds(pl.multiple_of(HALO + PLANE * i + 8 * h, 8), 8)
            at_j = pl.ds(ODD * i + 8 * h, 8)
            rho, u, v, w, pressure = [prims_a[m, at, :] for m in range(5)]
            scale = coef[rows, :]
            energy = 2.5 * pressure + 0.5 * rho * (u * u + v * v + w * w)
            before = [rho, rho * u, rho * v, rho * w, energy]
            after = [b + scale * whole_net(m, i, h, rows) for m, b in enumerate(before)]
            for m in range(5):
                half[m, rows, :] = 0.5 * (before[m] + after[m])
            vel = [after[m] / after[0] for m in (1, 2, 3)]
            speed_sq = vel[0] * vel[0] + vel[1] * vel[1] + vel[2] * vel[2]
            pressure = 0.4 * (after[4] - 0.5 * after[0] * speed_sq)
            for m, value in enumerate([after[0], *vel, pressure]):
                prims_b[m, at, :] = value
                prims_j[m, at_j, :] = value
        return carry

    def update_second(i, carry):
        for h in range(2):
            rows = pl.ds(pl.multiple_of(PLANE * i + 8 * h, 8), 8)
            scale = 0.5 * coef[rows, :]
            for m in range(5):
                result[m, rows, :] = half[m, rows, :] + scale * whole_net(m, i, h, rows)
        return carry

    def scale_rows(n, carry):
        rows = pl.ds(pl.multiple_of(8 * n, 8), 8)
        coef[rows, :] = (TIME_STEP / 12.0) * blank[rows, :].astype(F32) / volume[rows, :]
        return carry

    def stage(prims, copies, arrays, received, to_left, to_right, edges, wake, recv):
        sweep(1, put_j, 3, CELLS)
        for copy in copies:
            copy.wait_recv()
        wake.start()
        unpack_spans(arrays, *received)
        points_k(0, 3, 13, 3)
        points_k(3, 3 + CELLS, 14, 2)
        points_k(3 + CELLS, POINTS, 15, 3)
        sweep(2, put_k)
        finish_sides(to_left, to_right, edges)
        points_i(prims, 0, 3, 3)
        points_i(prims, 3 + CELLS, POINTS, 3)
        sweep(0, put_i)
        wake.wait_recv()
        unpack_wake(recv)
        points_wake()
        sweep(1, put_j, 0, 3)
        turn_back()
        drain_sides(to_left, to_right)
        for copy in copies:
            copy.wait_send()
        wake.wait_send()

    for load in loads[:4]:
        load.wait()
    turn(prims_a, spans, 5, HALO)
    turn(span_rows, span_metric, 3, 0)
    both = [(spans, 5), (span_metric, 3)]
    pack_spans(both, pack_up_a, pack_down_a)
    pl.semaphore_wait(barrier, 3 + has_left.astype(jnp.int32) + has_right.astype(jnp.int32))
    for copy in spans_1:
        copy.start()
    start_sides(to_left_a, to_right_a)
    for load in loads[4:]:
        load.wait()
    pack_wake(prims_a, wake_send_a)
    spread_rows(prims_a, HALO, prims_j, 5)
    spread_rows(normal, 0, normal_j, 3)
    lax.fori_loop(0, ROWS // 8, scale_rows, 0, unroll=4)
    points_j()
    points_i(prims_a, 3, 3 + CELLS, 2)
    stage(
        prims_a, spans_1, both, (below_a, above_a), to_left_a, to_right_a,
        [(prims_a, 5), (chord, 3)], wake_a, wake_recv_a,
    )
    lax.fori_loop(0, CELLS, update_first, 0)
    turn(prims_b, spans, 5, HALO)
    pack_spans([(spans, 5)], pack_up_b, pack_down_b)
    for copy in spans_2:
        copy.start()
    start_sides(to_left_b, to_right_b)
    pack_wake(prims_b, wake_send_b)
    points_j()
    points_i(prims_b, 3, 3 + CELLS, 2)
    stage(
        prims_b, spans_2, [(spans, 5)], (below_b, above_b), to_left_b, to_right_b,
        [(prims_b, 5)], wake_b, wake_recv_b,
    )
    lax.fori_loop(0, CELLS, update_second, 0, unroll=2)


def body(density, velocity, pressure, metrics, volume, wake_partner, iblank):
    flat = lambda array: array.reshape(array.shape[:-3] + (ROWS, LANES))
    memory = lambda *shape: pltpu.VMEM(shape, F32)
    anywhere = pl.BlockSpec(memory_space=pl.ANY)
    out = pl.pallas_call(
        kernel,
        out_shape=jax.ShapeDtypeStruct((5, ROWS, LANES), F32),
        in_specs=[anywhere] * 6 + [pl.BlockSpec(memory_space=pltpu.SMEM)],
        out_specs=pl.BlockSpec(memory_space=pltpu.VMEM),
        scratch_shapes=[
            memory(5, PADDED, LANES),
            memory(5, PADDED, LANES),
            memory(5, ODD * CELLS, LANES),
            memory(3, PADDED, LANES),
            memory(3, ROWS, LANES),
            memory(3, ODD * CELLS, LANES),
            memory(3, ROWS, LANES),
            memory(ROWS, LANES),
            pltpu.VMEM((ROWS, LANES), jnp.int32),
            memory(ROWS, LANES),
            memory(CELLS, PLANE, LANES),
            memory(CELLS, PLANE, LANES),
            memory(CELLS, PLANE, LANES),
            memory(CELLS, PLANE, LANES),
            memory(ODD * CELLS, LANES),
            memory(5, 2, SPAN_ROWS, LANES),
            memory(3, 2, SPAN_ROWS, LANES),
            memory(48, LANES),
            memory(48, LANES),
            memory(32, LANES),
            memory(32, LANES),
            memory(48, LANES),
            memory(48, LANES),
            memory(32, LANES),
            memory(32, LANES),
            memory(3, 20, 2 * POINTS, 8, LANES),
            memory(5, ROWS, LANES),
            memory(5, ODD * CELLS, LANES),
            memory(5, 2, ODD * 8, LANES),
            memory(5, ROWS, LANES),
            memory(5, ROWS, LANES),
            pltpu.SemaphoreType.DMA((8,)),
            pltpu.SemaphoreType.DMA((16,)),
            pltpu.SemaphoreType.DMA((16,)),
        ],
        compiler_params=pltpu.CompilerParams(
            collective_id=0, has_side_effects=True, vmem_limit_bytes=60 * 1024 * 1024
        ),
        name="weno_sections",
    )(
        flat(density), flat(velocity), flat(pressure), flat(metrics), flat(volume),
        flat(iblank), wake_partner,
    )
    return out.reshape(5, CELLS, PLANE, LANES)


def solution(mesh):
    placed = (
        P("wrap", None, "span"),
        P(None, "wrap", None, "span"),
        P("wrap", None, "span"),
        P(None, "wrap", None, "span"),
        P("wrap", None, "span"),
        P("wrap"),
        P("wrap", None, "span"),
    )
    return jax.shard_map(
        body, mesh=mesh, in_specs=placed, out_specs=P(None, "wrap", None, "span"), check_vma=False
    )
```

time: 46.7 us -> 39 us (0.84)
  Pallas kernels: 44.5 us -> 36.8 us
    pallas_call x1, Pallas kernels: 44.5 us -> 36.8 us  [body(): pl.pallas_call(kernel, out_shape=jax.ShapeDtypeStruct((5, ROWS, LANES), F...]
where the time goes in v1:
time: 39 us; the launch traced here: 38.8 us
  Pallas kernels  36.8 us (94%)
  local copies, waits for them, and re-layouts  1.99 us (5%)
    pallas_call x1, Pallas kernels, body(): pl.pallas_call(kernel, out_shape=jax.ShapeDtypeStruct((5, ROWS, LANES), F...  36.8 us
    unnamed x1, local copies, waits for them, and re-layouts  1.99 us

profile of v1, /device:TPU:1, one launch (start us, length us, event | category | flops | bytes accessed | tf_op | source)
XLA Modules:
  0.0 38.8 jit_solution(16447391449847139573)
XLA Ops:
  0.0 36.8 %weno_sections.1 = f32[5,256,128]{2,1,0:T(8,128)} custom-call(f32[256,128]{1,0:T(8,128)} %bitcast.10, f32[3,256,128]{2,1,0:T(8,128)} %bitcast.9, f32[256,128]{1,0:T(8,128)} %bitcast.11, f32[9,256,128]{2,1,0:T(8,128)} %bitcast.8, f32[256,128]{1,0:T(8,128)} %bitcast.12, s32[256,128]{1,0:T(8,128)} %bitcast.13, s32[16]{0:T(128)} %partner_ref.1), custom_call_target="tpu_custom_call" | custom-call | tf_op jit(solution)/shard_map/weno_sections/pallas_call | solution.py:477
  36.8 2.0 %copy.9 = f32[5,16,16,128]{3,2,1,0:T(8,128)} copy(f32[5,16,16,128]{3,2,1,0:T(8,128)} %bitcast.7) | data formatting | bytes 1310720
